TPU v7x, 32 devices: a whole 2x2x4 slice. The times are simulated.
32 devices in a mesh: row: 16 (over z, x, core), col: 2 (over y).
Axes of the slice: x: 2, y: 2, z: 4, core: 2. Of those that a mesh axis runs over, the one named last changes fastest.
Arguments:
- counts: int32 [8192, 32768], P('row', 'col'), may hold values from 0 to 63
- row_support: int32 [8192], P(('row', 'col')), may hold values from 1 to 2209
- col_support: int32 [32768], P(('col', 'row')), may hold values from 1 to 2209
- total: int32 [1], replicated, may hold values from 256 to 4095
- sketch: bfloat16 [32768, 256], P('col'), may hold values from -6 to 6
Outputs:
- left_basis: float32 [8192, 256], P('row')
- right_basis: float32 [32768, 256], P('col')
All inputs are finite; a program needn't handle non-finite values.
Results may differ from a plain program's by a relative error of at most 0.012.
Values may be sent and summed in bfloat16 or wider, within the bound.
A program may use at most 192 MiB of HBM per device.

v0:
```python
import jax
import jax.numpy as jnp
from jax import lax
from jax.sharding import PartitionSpec as P


def lift(block, row_part, col_part, total):
    value = jnp.log(jnp.maximum(block, 1).astype(jnp.float32))
    value = value + jnp.log(total[0].astype(jnp.float32))
    value = value - jnp.log(row_part.astype(jnp.float32))[:, None]
    value = value - jnp.log(col_part.astype(jnp.float32))[None, :]
    return jnp.where(block > 0, jnp.maximum(value, 0.0), 0.0).astype(jnp.bfloat16)


def factor_of(gram):
    return jnp.linalg.cholesky(gram)


def solve_rows(lower, matrix):
    return jax.scipy.linalg.solve_triangular(lower, matrix.T, lower=True).T


def gram_of(matrix):
    return jnp.dot(matrix.T, matrix, precision=lax.Precision.HIGHEST)


def per_device(counts, row_support, col_support, total, sketch):
    row_local = lax.all_gather(row_support, "col", axis=0, tiled=True)
    col_local = lax.all_gather(col_support, "row", axis=0, tiled=True)
    table = lift(counts, row_local, col_local, total)
    row_count = table.shape[0]
    col_count = table.shape[1]

    def left_orth(rhs, narrow):
        whole = lax.psum(jnp.dot(table, rhs, preferred_element_type=jnp.float32), "col")
        gram = lax.psum(gram_of(whole), "row")
        basis = solve_rows(factor_of(gram), whole)
        if narrow:
            return basis.astype(jnp.bfloat16)
        return basis

    q_first = left_orth(sketch, True)
    partial_value = lax.dot_general(
        table, q_first, (((0,), (0,)), ((), ())), preferred_element_type=jnp.float32
    )
    whole = lax.psum(partial_value, "row")
    gram = lax.psum(gram_of(whole), "col")
    q_second = solve_rows(factor_of(gram), whole)
    q_third = left_orth(q_second.astype(jnp.bfloat16), False)
    total_rows = row_count * lax.axis_size("row")
    total_cols = col_count * lax.axis_size("col")
    return (
        q_third * jnp.sqrt(jnp.float32(total_rows)),
        q_second * jnp.sqrt(jnp.float32(total_cols)),
    )


def solution(mesh):
    in_specs = (P("row", "col"), P(("row", "col")), P(("col", "row")), P(), P("col", None))
    out_specs = (P("row", None), P("col", None))
    return jax.shard_map(
        per_device, mesh=mesh, in_specs=in_specs, out_specs=out_specs, check_vma=False
    )
```

profile of v0, /device:TPU:0, one launch (start us, length us, event | category | flops | bytes accessed | tf_op | source)
XLA Modules:
  0.0 932.7 jit_solution(9221446948077840741)
XLA Ops:
  7.2 23.5 %all_gather.7 = s32[16384]{0:T(1024)S(1)} all-gather(s32[1024]{0:T(1024)} %param.10), channel_id=1, replica_groups=mesh['row'=16,'col'=2] {'row'}, dimensions={0}, use_global_device_ids=true | all-gather | bytes 69632 | tf_op jit(solution)/shard_map/all_gather | solution.py:29
  30.7 4.5 all-gather
  35.9 17.1 %select_convert_fusion = bf16[512,16384]{1,0:T(8,128)(2,1)S(1)} fusion(s32[512,16384]{1,0:T(8,128)} %param.8, f32[16384]{0:T(1024)S(1)} %convert_log_fusion, f32[512]{0:T(512)S(1)} %bitcast.119, f32[]{:T(128)} %bitcast), kind=kLoop, calls=%fused_computation.6 | loop fusion | flops 75497472 | bytes 50399236 | tf_op jit(solution)/shard_map/convert_element_type | solution.py:12
  53.0 6.2 copy-done.2
  59.2 7.7 fusion.42
  67.0 26.0 %all-reduce.8.cloned.1.call-done = f32[512,256]{1,0:T(8,128)} async-done(((f32[512,256]{1,0:T(8,128)}), f32[512,256]{1,0:T(8,128)}) %all-reduce.8.cloned.1.call-update) | async-done | bytes 524304 | tf_op jit(solution)/shard_map/psum | solution.py:35
  96.2 90.5 %all-reduce.10.cloned.1.call-done = f32[256,256]{0,1:T(8,128)} async-done(((f32[256,256]{0,1:T(8,128)}), f32[256,256]{0,1:T(8,128)}) %all-reduce.10.cloned.1.call-update) | async-done | bytes 262160 | tf_op jit(solution)/shard_map/psum | solution.py:36
  188.8 11.7 %cholesky.172 = f32[128,128]{1,0:T(8,128)S(1)} custom-call(f32[128,128]{1,0:T(8,128)S(1)} %cholesky.270), custom_call_target="Cholesky" | custom-call | tf_op jit(solution)/shard_map/jit(cholesky)/cholesky | solution.py:16
  200.6 9.8 %custom-call.19 = f32[1,128,128]{1,2,0:T(8,128)S(1)} custom-call(f32[1,128,128]{2,1,0:T(8,128)S(1)} %get-tuple-element.73), custom_call_target="InvertDiagBlocksLowerTriangular" | custom-call | tf_op jit(solution)/shard_map/jit(cholesky)/cholesky | solution.py:16
  210.9 11.7 %cholesky.189 = f32[128,128]{1,0:T(8,128)S(1)} custom-call(f32[128,128]{1,0:T(8,128)S(1)} %convolution_subtract_fusion.5), custom_call_target="Cholesky" | custom-call | tf_op jit(solution)/shard_map/jit(cholesky)/cholesky | solution.py:16
  224.9 4.5 while.6
  229.4 19.7 %custom-call.20 = f32[2,128,128]{1,2,0:T(8,128)S(1)} custom-call(f32[2,128,128]{2,1,0:T(8,128)S(1)} %get-tuple-element.26), custom_call_target="InvertDiagBlocksLowerTriangular" | custom-call | tf_op jit(solution)/shard_map/jit(_solve_triangular)/triangular_solve | solution.py:20
  252.4 16.1 %fusion.6 = f32[16384,256]{1,0:T(8,128)} fusion(bf16[512,16384]{1,0:T(8,128)(2,1)} %copy-done.2, bf16[128,512]{1,0:T(8,128)(2,1)S(1)} %fusion.23, f32[128,512]{1,0:T(8,128)S(1)} %fusion.9), kind=kOutput, calls=%fused_computation.25 | convolution fusion | flops 4295491584 | bytes 33947648 | tf_op jit(solution)/shard_map/dot_general | solution.py:43
  268.6 298.5 %all-reduce.12.cloned.1.call-done = f32[16384,256]{1,0:T(8,128)} async-done(((f32[16384,256]{1,0:T(8,128)}), f32[16384,256]{1,0:T(8,128)}) %all-reduce.12.cloned.1.call-update) | async-done | bytes 16777232 | tf_op jit(solution)/shard_map/psum | solution.py:46
  567.1 37.8 %fusion.44 = f32[256,256]{0,1:T(8,128)} fusion(f32[16384,256]{1,0:T(8,128)} %all-reduce.12.cloned.1.call-done), kind=kOutput, calls=%fused_computation.95 | convolution fusion | flops 12884901888 | bytes 17039360 | tf_op jit(solution)/shard_map/dot_general | solution.py:24
  605.0 23.0 %all-reduce.14.cloned.1.call-done = f32[256,256]{0,1:T(8,128)} async-done(((f32[256,256]{0,1:T(8,128)}), f32[256,256]{0,1:T(8,128)}) %all-reduce.14.cloned.1.call-update) | async-done | bytes 262160 | tf_op jit(solution)/shard_map/psum | solution.py:47
  630.1 11.7 %cholesky.206 = f32[128,128]{1,0:T(8,128)S(1)} custom-call(f32[128,128]{1,0:T(8,128)S(1)} %cholesky.273), custom_call_target="Cholesky" | custom-call | tf_op jit(solution)/shard_map/jit(cholesky)/cholesky | solution.py:16
  641.9 9.8 %custom-call.21 = f32[1,128,128]{1,2,0:T(8,128)S(1)} custom-call(f32[1,128,128]{2,1,0:T(8,128)S(1)} %get-tuple-element.69), custom_call_target="InvertDiagBlocksLowerTriangular" | custom-call | tf_op jit(solution)/shard_map/jit(cholesky)/cholesky | solution.py:16
  652.2 11.7 %cholesky.223 = f32[128,128]{1,0:T(8,128)S(1)} custom-call(f32[128,128]{1,0:T(8,128)S(1)} %convolution_subtract_fusion.4), custom_call_target="Cholesky" | custom-call | tf_op jit(solution)/shard_map/jit(cholesky)/cholesky | solution.py:16
  670.3 19.7 %custom-call.15 = f32[2,128,128]{1,2,0:T(8,128)S(1)} custom-call(f32[2,128,128]{2,1,0:T(8,128)S(1)} %get-tuple-element.19), custom_call_target="InvertDiagBlocksLowerTriangular" | custom-call | tf_op jit(solution)/shard_map/jit(_solve_triangular)/triangular_solve | solution.py:20
  690.0 10.8 %fusion.3 = f32[128,16384]{1,0:T(8,128)S(1)} fusion(f32[256,16384]{0,1:T(8,128)} %bitcast.113, f32[2,128,128]{1,2,0:T(8,128)S(1)} %custom-call.15), kind=kOutput, calls=%fused_computation.12 | convolution fusion | flops 3221225472 | bytes 16842752 | tf_op jit(solution)/shard_map/jit(_solve_triangular)/triangular_solve | solution.py:20
  700.8 13.4 %convolution_subtract_fusion = f32[128,16384]{0,1:T(8,128)S(1)} fusion(f32[128,16384]{1,0:T(8,128)S(1)} %fusion.3, f32[256,16384]{0,1:T(8,128)S(1)} %bitcast.114, f32[256,256]{1,0:T(8,128)S(1)} %get-tuple-element.225), kind=kOutput, calls=%fused_computation.7 | convolution fusion | flops 3223322624 | bytes 25231360 | tf_op jit(solution)/shard_map/jit(_solve_triangular)/triangular_solve | solution.py:20
  714.2 9.8 %fusion.19 = f32[128,16384]{1,0:T(8,128)} fusion(f32[128,16384]{0,1:T(8,128)S(1)} %convolution_subtract_fusion, f32[2,128,128]{1,2,0:T(8,128)S(1)} %custom-call.15), kind=kOutput, calls=%fused_computation.45 | convolution fusion | flops 3221225472 | bytes 16842752 | tf_op jit(solution)/shard_map/jit(_solve_triangular)/triangular_solve | solution.py:20
  724.0 13.7 %fusion.1 = f32[512,256]{1,0:T(8,128)} fusion(bf16[512,16384]{1,0:T(8,128)(2,1)} %copy-done.2, f32[128,16384]{1,0:T(8,128)} %fusion.19, f32[128,16384]{1,0:T(8,128)} %copy-done.1), kind=kOutput, calls=%fused_computation.11 | convolution fusion | flops 4311744512 | bytes 34078720 | tf_op jit(solution)/shard_map/dot_general | solution.py:35
  737.8 28.8 %all-reduce.16.cloned.1.call-done = f32[512,256]{1,0:T(8,128)} async-done(((f32[512,256]{1,0:T(8,128)}), f32[512,256]{1,0:T(8,128)}) %all-reduce.16.cloned.1.call-update) | async-done | bytes 524304 | tf_op jit(solution)/shard_map/psum | solution.py:35
  769.5 12.1 %multiply_bitcast_fusion = f32[16384,256]{0,1:T(8,128)} fusion(f32[128,16384]{1,0:T(8,128)} %fusion.19, f32[128,16384]{1,0:T(8,128)} %copy-done.1), kind=kLoop, calls=%fused_computation.9 | loop fusion | flops 8388608 | bytes 33554432 | tf_op jit(solution)/shard_map/mul | solution.py:54
  781.6 17.5 %copy.22 = f32[16384,256]{1,0:T(8,128)} copy(f32[16384,256]{0,1:T(8,128)} %multiply_bitcast_fusion) | data formatting | bytes 33554432
  799.2 61.0 %all-reduce.18.cloned.1.call-done = f32[256,256]{0,1:T(8,128)} async-done(((f32[256,256]{0,1:T(8,128)}), f32[256,256]{0,1:T(8,128)}) %all-reduce.18.cloned.1.call-update) | async-done | bytes 262160 | tf_op jit(solution)/shard_map/psum | solution.py:36
  862.2 11.7 %cholesky.240 = f32[128,128]{1,0:T(8,128)S(1)} custom-call(f32[128,128]{1,0:T(8,128)S(1)} %cholesky.276), custom_call_target="Cholesky" | custom-call | tf_op jit(solution)/shard_map/jit(cholesky)/cholesky | solution.py:16
  874.0 9.8 %custom-call.22 = f32[1,128,128]{1,2,0:T(8,128)S(1)} custom-call(f32[1,128,128]{2,1,0:T(8,128)S(1)} %get-tuple-element.65), custom_call_target="InvertDiagBlocksLowerTriangular" | custom-call | tf_op jit(solution)/shard_map/jit(cholesky)/cholesky | solution.py:16
  884.3 11.7 %cholesky.257 = f32[128,128]{1,0:T(8,128)S(1)} custom-call(f32[128,128]{1,0:T(8,128)S(1)} %convolution_subtract_fusion.3), custom_call_target="Cholesky" | custom-call | tf_op jit(solution)/shard_map/jit(cholesky)/cholesky | solution.py:16
  902.9 20.0 %custom-call.23 = f32[2,128,128]{1,2,0:T(8,128)S(1)} custom-call(f32[2,128,128]{2,1,0:T(8,128)S(1)} %get-tuple-element.27), custom_call_target="InvertDiagBlocksLowerTriangular" | custom-call | tf_op jit(solution)/shard_map/jit(_solve_triangular)/triangular_solve | solution.py:20
  (88 shorter events, 43.5 us)
Async XLA Ops:
  7.2 85.9 %all-reduce.8.cloned.1.call-start = ((), (), s32[]{:S(2)}) async-start(), calls=%async_computation | async-start | bytes 1048576 | tf_op jit(solution)/shard_map/psum | solution.py:35
  53.0 6.2 copy-start.2
  67.0 119.8 %all-reduce.10.cloned.1.call-start = ((), (), s32[]{:S(2)}) async-start(), calls=%async_computation.1 | async-start | bytes 524288 | tf_op jit(solution)/shard_map/psum | solution.py:36
  96.0 471.1 %all-reduce.12.cloned.1.call-start = ((), (), s32[]{:S(2)}) async-start(), calls=%async_computation.2 | async-start | bytes 33554432 | tf_op jit(solution)/shard_map/psum | solution.py:46
  268.5 359.5 %all-reduce.14.cloned.1.call-start = ((), (), s32[]{:S(2)}) async-start(), calls=%async_computation.3 | async-start | bytes 524288 | tf_op jit(solution)/shard_map/psum | solution.py:47
  605.0 161.6 %all-reduce.16.cloned.1.call-start = ((), (), s32[]{:S(2)}) async-start(), calls=%async_computation.4 | async-start | bytes 1048576 | tf_op jit(solution)/shard_map/psum | solution.py:35
  690.0 10.8 %copy-start = (f32[16384,256]{1,0:T(8,128)S(1)}, f32[16384,256]{1,0:T(8,128)}, u32[]{:S(2)}) copy-start(f32[16384,256]{1,0:T(8,128)} %all-reduce.12.cloned.1.call-done) | copy-start | bytes 50331652
  700.8 13.4 %copy-start.1 = (f32[128,16384]{1,0:T(8,128)}, f32[128,16384]{1,0:T(8,128)S(1)}, u32[]{:S(2)}) copy-start(f32[128,16384]{1,0:T(8,128)S(1)} %fusion.3) | copy-start | bytes 25165828
  737.7 122.4 %all-reduce.18.cloned.1.call-start = ((), (), s32[]{:S(2)}) async-start(), calls=%async_computation.5 | async-start | bytes 524288 | tf_op jit(solution)/shard_map/psum | solution.py:36
  781.6 141.2 %copy-start.3 = (f32[512,256]{1,0:T(8,128)S(1)}, f32[512,256]{1,0:T(8,128)}, u32[]{:S(2)}) copy-start(f32[512,256]{1,0:T(8,128)} %all-reduce.16.cloned.1.call-done) | copy-start | bytes 1572868
Sparse Core Ops, SparseCore 0:
  67.1 25.9 all-reduce.7
  97.0 89.7 all-reduce.9
  268.7 298.4 all-reduce.11
  605.1 22.9 all-reduce.13
  737.9 28.6 all-reduce.15
  770.4 89.6 all-reduce.17
where the time goes:
time: 938 us; the launch traced here: 933 us
  waiting for transfers between devices  528 us (56%)
  other arithmetic  195 us (21%)
  matrix products  121 us (13%)
  local copies, waits for them, and re-layouts  40 us (4%)
  blocking collectives  28 us (3%)
  between operations  19.6 us (2%)
    psum x1, waiting for transfers between devices, per_device(): whole = lax.psum(partial_value, 'row')  299 us
    psum x2, waiting for transfers between devices, left_orth(): gram = lax.psum(gram_of(whole), 'row')  151 us
    another operation x20, other arithmetic, factor_of(): return jnp.linalg.cholesky(gram)  103 us
    another operation x7, other arithmetic, solve_rows(): return jax.scipy.linalg.solve_triangular(lower, matrix.T, lower=True).T  59.4 us
    psum x2, waiting for transfers between devices, left_orth(): lax.psum(jnp.dot(table, rhs, preferred_element_type=jnp.float32), 'col')  54.8 us
    dot_general x3, matrix products, gram_of(): return jnp.dot(matrix.T, matrix, precision=lax.Precision.HIGHEST)  43.6 us
    another operation x9, matrix products, solve_rows(): return jax.scipy.linalg.solve_triangular(lower, matrix.T, lower=True).T  38.7 us
    unnamed x10, local copies, waits for them, and re-layouts  24.7 us
  transfers between devices with their start and end apart: 6, of which 6 were waited for; matrix products, arithmetic and copies ran while one was open for 3% of the time, Pallas kernels for 0%

commit v1 on v0

--- a/solution.py
+++ b/solution.py
@@ -43,7 +43,9 @@
     partial_value = lax.dot_general(
         table, q_first, (((0,), (0,)), ((), ())), preferred_element_type=jnp.float32
     )
-    whole = lax.psum(partial_value, "row")
+    whole = partial_value
+    for hop in (1, 2, 4, 8):
+        whole = whole + lax.ppermute(whole, "row", [(dev, dev ^ hop) for dev in range(16)])
     gram = lax.psum(gram_of(whole), "col")
     q_second = solve_rows(factor_of(gram), whole)
     q_third = left_orth(q_second.astype(jnp.bfloat16), False)

time: 938 us -> 2150 us (2.29)
  waiting for transfers between devices: 528 us -> 1680 us
  other arithmetic: 195 us -> 248 us
    ppermute x0 -> x4, waiting for transfers between devices: none -> 1470 us  [per_device(): lax.ppermute(whole, 'row', [(dev, dev ^ hop) for dev in range(16)])]
    psum x1 -> x0, waiting for transfers between devices: 299 us -> none  [per_device(): whole = lax.psum(partial_value, 'row')]
    add x0 -> x3, other arithmetic: none -> 34.9 us  [per_device(): whole + lax.ppermute(whole, 'row', [(dev, dev ^ hop) for dev in range(16)])]
  transfers between devices with their start and end apart: 6 -> 9, of which waited for: 6 -> 9; matrix products, arithmetic and copies ran while one was open for 3% -> 2% of each run, Pallas kernels for 0% -> 0%
where the time goes in v1:
time: 2150 us; the launch traced here: 2140 us
  waiting for transfers between devices  1680 us (78%)
  other arithmetic  248 us (12%)
  matrix products  118 us (5%)
  local copies, waits for them, and re-layouts  43.5 us (2%)
  blocking collectives  28 us (1%)
    ppermute x4, waiting for transfers between devices, per_device(): lax.ppermute(whole, 'row', [(dev, dev ^ hop) for dev in range(16)])  1470 us
    psum x2, waiting for transfers between devices, left_orth(): gram = lax.psum(gram_of(whole), 'row')  152 us
    another operation x20, other arithmetic, factor_of(): return jnp.linalg.cholesky(gram)  103 us
    another operation x7, other arithmetic, solve_rows(): return jax.scipy.linalg.solve_triangular(lower, matrix.T, lower=True).T  59.8 us
    psum x2, waiting for transfers between devices, left_orth(): lax.psum(jnp.dot(table, rhs, preferred_element_type=jnp.float32), 'col')  54.8 us
    dot_general x3, matrix products, gram_of(): return jnp.dot(matrix.T, matrix, precision=lax.Precision.HIGHEST)  48.2 us
  transfers between devices with their start and end apart: 9, of which 9 were waited for; matrix products, arithmetic and copies ran while one was open for 2% of the time, Pallas kernels for 0%

profile of v1, /device:TPU:0, one launch (start us, length us, event | category | flops | bytes accessed | tf_op | source)
XLA Modules:
  0.0 2141.1 jit_solution(7547308335067274617)
XLA Ops:
  13.4 22.5 %all_gather.7 = s32[16384]{0:T(1024)S(1)} all-gather(s32[1024]{0:T(1024)} %param.10), channel_id=1, replica_groups=mesh['row'=16,'col'=2] {'row'}, dimensions={0}, use_global_device_ids=true | all-gather | bytes 69632 | tf_op jit(solution)/shard_map/all_gather | solution.py:29
  35.9 17.1 select_convert_fusion
  67.0 26.0 %all-reduce.7.cloned.1.call-done = f32[512,256]{1,0:T(8,128)} async-done(((f32[512,256]{1,0:T(8,128)}), f32[512,256]{1,0:T(8,128)}) %all-reduce.7.cloned.1.call-update) | async-done | bytes 524304 | tf_op jit(solution)/shard_map/psum | solution.py:35
  96.2 90.6 %all-reduce.9.cloned.1.call-done = f32[256,256]{0,1:T(8,128)} async-done(((f32[256,256]{0,1:T(8,128)}), f32[256,256]{0,1:T(8,128)}) %all-reduce.9.cloned.1.call-update) | async-done | bytes 262160 | tf_op jit(solution)/shard_map/psum | solution.py:36
  188.8 11.7 cholesky.172
  200.6 9.8 custom-call.19
  210.9 11.7 cholesky.189
  229.2 19.7 custom-call.20
  261.0 24.9 %collective-permute-done = f32[16384,256]{1,0:T(8,128)} collective-permute-done((f32[16384,256]{1,0:T(8,128)S(1)}, f32[16384,256]{1,0:T(8,128)}, u32[]{:S(2)}, u32[]{:S(2)}) %collective-permute-start) | collective-permute-done | bytes 16777248 | tf_op jit(solution)/shard_map/ppermute | solution.py:48
  285.9 11.7 add.51
  298.2 362.2 %collective-permute-done.1 = f32[16384,256]{1,0:T(8,128)} collective-permute-done((f32[16384,256]{1,0:T(8,128)}, f32[16384,256]{1,0:T(8,128)}, u32[]{:S(2)}, u32[]{:S(2)}) %collective-permute-start.1) | collective-permute-done | bytes 16777248 | tf_op jit(solution)/shard_map/ppermute | solution.py:48
  660.4 11.4 add.52
  674.5 359.8 %collective-permute-done.2 = f32[16384,256]{1,0:T(8,128)} collective-permute-done((f32[16384,256]{1,0:T(8,128)S(1)}, f32[16384,256]{1,0:T(8,128)}, u32[]{:S(2)}, u32[]{:S(2)}) %collective-permute-start.2) | collective-permute-done | bytes 16777248 | tf_op jit(solution)/shard_map/ppermute | solution.py:48
  1034.3 11.7 add.53
  1047.8 719.8 %collective-permute-done.3 = f32[16384,256]{1,0:T(8,128)} collective-permute-done((f32[16384,256]{1,0:T(8,128)}, f32[16384,256]{1,0:T(8,128)}, u32[]{:S(2)}, u32[]{:S(2)}) %collective-permute-start.3) | collective-permute-done | bytes 16777248 | tf_op jit(solution)/shard_map/ppermute | solution.py:48
  1767.6 42.4 %fusion.6 = f32[256,256]{0,1:T(8,128)} fusion(f32[16384,256]{1,0:T(8,128)} %add.53, f32[16384,256]{1,0:T(8,128)} %collective-permute-done.3), kind=kOutput, calls=%fused_computation.16 | convolution fusion | flops 12889096192 | bytes 33816576 | tf_op jit(solution)/shard_map/dot_general | solution.py:24
  1810.1 18.1 add_bitcast_fusion
  1834.6 11.7 cholesky.206
  1847.0 9.8 custom-call.21
  1857.3 11.7 cholesky.223
  1875.3 20.1 custom-call.15
  1895.4 10.6 fusion.4
  1909.2 13.3 fusion.21
  1922.6 10.3 fusion.3
  1932.9 13.7 fusion.1
  1946.7 28.8 %all-reduce.13.cloned.1.call-done = f32[512,256]{1,0:T(8,128)} async-done(((f32[512,256]{1,0:T(8,128)}), f32[512,256]{1,0:T(8,128)}) %all-reduce.13.cloned.1.call-update) | async-done | bytes 524304 | tf_op jit(solution)/shard_map/psum | solution.py:35
  1978.4 12.1 multiply_bitcast_fusion
  1990.5 17.5 copy.22
  2008.0 61.0 %all-reduce.15.cloned.1.call-done = f32[256,256]{0,1:T(8,128)} async-done(((f32[256,256]{0,1:T(8,128)}), f32[256,256]{0,1:T(8,128)}) %all-reduce.15.cloned.1.call-update) | async-done | bytes 262160 | tf_op jit(solution)/shard_map/psum | solution.py:36
  2071.1 11.7 cholesky.240
  2093.8 11.7 cholesky.257
  2111.8 19.9 custom-call.23
  (104 shorter events, 98.8 us)
Async XLA Ops:
  7.2 85.9 %all-reduce.7.cloned.1.call-start = ((), (), s32[]{:S(2)}) async-start(), calls=%async_computation | async-start | bytes 1048576 | tf_op jit(solution)/shard_map/psum | solution.py:35
  53.0 6.2 copy-start.1
  67.0 119.8 %all-reduce.9.cloned.1.call-start = ((), (), s32[]{:S(2)}) async-start(), calls=%async_computation.1 | async-start | bytes 524288 | tf_op jit(solution)/shard_map/psum | solution.py:36
  96.0 1736.5 %all-reduce.11.cloned.1.call-start = ((), (), s32[]{:S(2)}) async-start(), calls=%async_computation.2 | async-start | bytes 524288 | tf_op jit(solution)/shard_map/psum | solution.py:49
  260.5 25.4 %collective-permute-start = (f32[16384,256]{1,0:T(8,128)S(1)}, f32[16384,256]{1,0:T(8,128)}, u32[]{:S(2)}, u32[]{:S(2)}) collective-permute-start(f32[16384,256]{1,0:T(8,128)S(1)} %fusion.9), channel_id=1, source_target_pairs={{0,2},{2,0},{4,6},{6,4},{8,10},{10,8},{12,14},{14,12},{16,18},{18,... | collective-permute-start | bytes 50331656 | tf_op jit(solution)/shard_map/ppermute | solution.py:48
  297.6 362.8 %collective-permute-start.1 = (f32[16384,256]{1,0:T(8,128)}, f32[16384,256]{1,0:T(8,128)}, u32[]{:S(2)}, u32[]{:S(2)}) collective-permute-start(f32[16384,256]{1,0:T(8,128)} %add.51), channel_id=1, source_target_pairs={{0,4},{2,6},{4,0},{6,2},{8,12},{10,14},{12,8},{14,10},{16,20},{18,... | collective-permute-start | bytes 50331656 | tf_op jit(solution)/shard_map/ppermute | solution.py:48
  671.9 362.4 %collective-permute-start.2 = (f32[16384,256]{1,0:T(8,128)S(1)}, f32[16384,256]{1,0:T(8,128)}, u32[]{:S(2)}, u32[]{:S(2)}) collective-permute-start(f32[16384,256]{1,0:T(8,128)S(1)} %add.52), channel_id=1, source_target_pairs={{0,8},{2,10},{4,12},{6,14},{8,0},{10,2},{12,4},{14,6},{16,24},{18,... | collective-permute-start | bytes 50331656 | tf_op jit(solution)/shard_map/ppermute | solution.py:48
  1046.0 721.6 %collective-permute-start.3 = (f32[16384,256]{1,0:T(8,128)}, f32[16384,256]{1,0:T(8,128)}, u32[]{:S(2)}, u32[]{:S(2)}) collective-permute-start(f32[16384,256]{1,0:T(8,128)} %add.53), channel_id=1, source_target_pairs={{0,16},{2,18},{4,20},{6,22},{8,24},{10,26},{12,28},{14,30},{16,0},... | collective-permute-start | bytes 50331656 | tf_op jit(solution)/shard_map/ppermute | solution.py:48
  1810.0 165.5 %all-reduce.13.cloned.1.call-start = ((), (), s32[]{:S(2)}) async-start(), calls=%async_computation.3 | async-start | bytes 1048576 | tf_op jit(solution)/shard_map/psum | solution.py:35
  1895.4 27.2 %slice-start = ((s8[16777216]{0:T(1024)(128)(4,1)}), s8[4194304]{0:T(1024)(128)(4,1)S(1)}, s32[]{:S(2)}) async-start(s8[16777216]{0:T(1024)(128)(4,1)} %bitcast.111), calls=%async_computation.5 | async-start | bytes 8388608
  1895.4 27.2 %slice-start.1 = ((s8[16777216]{0:T(1024)(128)(4,1)}), s8[4194304]{0:T(1024)(128)(4,1)S(1)}, s32[]{:S(2)}) async-start(s8[16777216]{0:T(1024)(128)(4,1)} %bitcast.111), calls=%async_computation.6 | async-start | bytes 8388608
  1906.0 3.2 copy-start
  1909.2 13.4 slice-start.2
  1909.2 13.4 slice-start.3
  1946.7 122.4 %all-reduce.15.cloned.1.call-start = ((), (), s32[]{:S(2)}) async-start(), calls=%async_computation.4 | async-start | bytes 524288 | tf_op jit(solution)/shard_map/psum | solution.py:36
  1990.5 141.2 %copy-start.2 = (f32[512,256]{1,0:T(8,128)S(1)}, f32[512,256]{1,0:T(8,128)}, u32[]{:S(2)}) copy-start(f32[512,256]{1,0:T(8,128)} %all-reduce.13.cloned.1.call-done) | copy-start | bytes 1572868
Sparse Core Ops, SparseCore 0:
  67.1 25.9 all-reduce.6
  97.0 89.7 all-reduce.8
  1810.1 22.3 all-reduce.10
  1946.8 28.6 all-reduce.12
  1979.3 89.6 all-reduce.14
